TPU v7x, 256 devices: a whole 4x4x8 slice. The times are simulated.
256 devices in a mesh: dp: 32 (over z, y), seq: 8 (over x, core).
Axes of the slice: x: 4, y: 4, z: 8, core: 2. Of those that a mesh axis runs over, the one named last changes fastest.
Arguments:
- slot_tokens: bfloat16 [416, 512, 1152], P('dp', 'seq'), may hold values from -12 to 12
- modulation: float32 [32, 6, 1152], P('dp'), may hold values from -2.5 to 2.5
- counts: int32 [32], replicated, may hold values from 1 to 13, as said below
- dest: int32 [32, 13], replicated, may hold values from 0 to 223, as said below
- qkv_spatial: bfloat16 [1152, 1728], replicated, may hold values from -4 to 4
- out_spatial: bfloat16 [576, 1152], replicated, may hold values from -0.25 to 0.25
- qkv_temporal: bfloat16 [1152, 1728], replicated, may hold values from -4 to 4
- out_temporal: bfloat16 [576, 1152], replicated, may hold values from -0.25 to 0.25
Outputs:
- video_out: bfloat16 [224, 512, 1152], P('dp', 'seq')
Inputs may be any that keep to these rules, and one draw needn't show every extreme that they name: Group g holds blocks in slots 0 to counts[g] - 1; the counts sum to 224; some group holds 13 blocks. Over the slots q below counts[g] of all groups g, dest[g, q] takes every value 0 to 223 exactly once; one group sends at most 1 block to one video, and some group sends 1; entries at slots from counts[g] on are arbitrary values of the same range.
All inputs are finite; a program needn't handle non-finite values.
Results may differ from a plain program's by a relative error of at most 0.0057.
Values may be sent and summed in bfloat16 or wider, within the bound.
No kernel may reach another device: no remote copies, remote signals or barrier semaphores. Data moves between devices by JAX's collectives and lax.ppermute only.
A program may use at most 64 MiB of HBM per device.

v0:
```python
import math
import jax
import jax.numpy as jnp
from jax import lax
from jax.sharding import PartitionSpec as P

HEADS = 8
HEAD_DIM = 72
NFD = 7
epsilon = 1e-06


def norm_mod(tokens, shift_row, scale_row):
    values = tokens.astype(jnp.float32)
    center = values - jnp.mean(values, axis=-1, keepdims=True)
    spread = jnp.mean(center * center, axis=-1, keepdims=True)
    return (center * lax.rsqrt(spread + epsilon) * (1.0 + scale_row) + shift_row).astype(
        jnp.bfloat16
    )


def attention(qkv_rows, batch_count, length):
    parts = qkv_rows.reshape(batch_count, length, 3, HEADS, HEAD_DIM)
    factor = 1.0 / math.sqrt(HEAD_DIM)
    scores = (
        jnp.einsum(
            "bqhs,bkhs->bhqk", parts[:, :, 0], parts[:, :, 1], preferred_element_type=jnp.float32
        )
        * factor
    )
    highest = jnp.max(scores, axis=-1, keepdims=True)
    raised = jnp.exp(scores - highest)
    weights = (raised / jnp.sum(raised, axis=-1, keepdims=True)).astype(jnp.bfloat16)
    mixed = jnp.einsum(
        "bhqk,bkhs->bqhs", weights, parts[:, :, 2], preferred_element_type=jnp.float32
    )
    return mixed.astype(jnp.bfloat16).reshape(batch_count * length, HEADS * HEAD_DIM)


def spatial_block(frames, modulation_rows, w_qkv, w_out):
    frame_count, patch_count, model_width = frames.shape
    shift_rows = modulation_rows[:, 0][:, None, :]
    scale_rows = modulation_rows[:, 1][:, None, :]
    gate_rows = modulation_rows[:, 2][:, None, :]
    normed = norm_mod(frames, shift_rows, scale_rows)
    qkv_rows = jnp.dot(
        normed.reshape(-1, model_width), w_qkv, preferred_element_type=jnp.float32
    ).astype(jnp.bfloat16)
    mixed = attention(qkv_rows, frame_count, patch_count)
    projected = jnp.dot(mixed, w_out, preferred_element_type=jnp.float32).reshape(
        frame_count, patch_count, model_width
    )
    return (frames.astype(jnp.float32) + gate_rows * projected).astype(jnp.bfloat16)


def on_device(
    slot_tokens, modulation, counts, dest, qkv_spatial, out_spatial, qkv_temporal, out_temporal
):
    group_count = lax.axis_size("dp")
    slot_count, patch_count, model_width = slot_tokens.shape
    block_count = NFD
    send_room = (slot_count + group_count - 1) // group_count
    group_index = lax.axis_index("dp")
    slot_ids = jnp.arange(slot_count, dtype=jnp.int32)
    group_ids = jnp.arange(group_count, dtype=jnp.int32)
    room_ids = jnp.arange(send_room, dtype=jnp.int32)
    live_slots = slot_ids[None, :] < counts[:, None]
    target_group = dest // block_count
    earlier = slot_ids[:, None] < slot_ids[None, :]
    same_target = (
        live_slots[:, :, None]
        & (target_group[:, :, None] == target_group[:, None, :])
        & earlier[None, :, :]
    )
    send_rank = jnp.sum(same_target.astype(jnp.int32), axis=1)
    own_live = lax.dynamic_index_in_dim(
        live_slots.astype(jnp.int32), group_index, 0, keepdims=False
    )
    own_target = lax.dynamic_index_in_dim(target_group, group_index, 0, keepdims=False)
    own_rank = lax.dynamic_index_in_dim(send_rank, group_index, 0, keepdims=False)
    picks = (
        (own_live[:, None, None] > 0)
        & (own_target[:, None, None] == group_ids[None, :, None])
        & (own_rank[:, None, None] == room_ids[None, None, :])
    )
    chosen_slot = jnp.sum(picks.astype(jnp.int32) * slot_ids[:, None, None], axis=0).reshape(-1)
    video_rows = lax.all_gather(modulation, "dp", axis=0, tiled=True)
    slot_modulation = jnp.take(video_rows, own_target, axis=0)
    processed = spatial_block(slot_tokens, slot_modulation, qkv_spatial, out_spatial)
    payload = jnp.take(processed, chosen_slot, axis=0)
    arrived = lax.all_to_all(payload, "dp", split_axis=0, concat_axis=0, tiled=True)
    wanted = group_index * block_count + jnp.arange(block_count, dtype=jnp.int32)
    matches = (live_slots[:, :, None] & (dest[:, :, None] == wanted[None, None, :])).astype(
        jnp.int32
    )
    source_group = jnp.sum(matches * group_ids[:, None, None], axis=(0, 1))
    source_rank = jnp.sum(matches * send_rank[:, :, None], axis=(0, 1))
    placed = jnp.take(arrived, source_group * send_room + source_rank, axis=0)
    own_modulation = modulation[0]
    shard_count = lax.axis_size("seq")
    widest = patch_count // shard_count
    frame_total = shard_count * block_count
    channels = placed.shape[-1]
    selected = placed.reshape(block_count, shard_count, widest, channels)
    moved = lax.all_to_all(selected, "seq", split_axis=1, concat_axis=0, tiled=True)
    token_rows = moved.reshape(frame_total * widest, channels)
    normed_rows = norm_mod(token_rows, own_modulation[3], own_modulation[4])
    qkv_rows = jnp.dot(normed_rows, qkv_temporal, preferred_element_type=jnp.float32).astype(
        jnp.bfloat16
    )
    qkv_width = qkv_rows.shape[-1]
    by_patch = (
        qkv_rows.reshape(frame_total, widest, qkv_width)
        .transpose(1, 0, 2)
        .reshape(widest * frame_total, qkv_width)
    )
    mixed = attention(by_patch, widest, frame_total)
    attn_width = mixed.shape[-1]
    mixed = (
        mixed.reshape(widest, frame_total, attn_width)
        .transpose(1, 0, 2)
        .reshape(frame_total * widest, attn_width)
    )
    projected_rows = jnp.dot(mixed, out_temporal, preferred_element_type=jnp.float32)
    homeward = (token_rows.astype(jnp.float32) + own_modulation[5] * projected_rows).astype(
        jnp.bfloat16
    )
    back_width = homeward.shape[-1]
    returned = lax.all_to_all(
        homeward.reshape(frame_total, 1, widest, back_width),
        "seq",
        split_axis=0,
        concat_axis=1,
        tiled=True,
    )
    restored = returned.reshape(block_count, patch_count, back_width)
    return restored


def solution(mesh):
    in_specs = (P("dp", "seq", None), P("dp", None, None), P(), P(), P(), P(), P(), P())
    out_specs = P("dp", "seq", None)
    return jax.shard_map(
        on_device, mesh=mesh, in_specs=in_specs, out_specs=out_specs, check_vma=False
    )
```

profile of v0, /device:TPU:1, one launch (start us, length us, event | category | flops | bytes accessed | tf_op | source)
XLA Modules:
  0.0 281.3 jit_solution(13004928788901511606)
XLA Ops:
  0.0 0.9 add_select_fusion
  3.0 47.9 %all_gather.3 = f32[32,6,1152]{2,1,0:T(8,128)} all-gather(f32[1,6,1152]{2,1,0:T(8,128)S(1)} %copy.83), channel_id=1, replica_groups=mesh['dp'=32,'seq'=8] {'dp'}, dimensions={0}, use_global_device_ids=true | all-gather | bytes 912384 | tf_op jit(solution)/shard_map/all_gather | solution.py:87
  50.9 2.6 gather_fusion
  53.5 1.1 broadcast_select_fusion.1
  55.8 1.0 fusion.7
  56.8 1.1 copy-done.6
  57.9 5.4 %convolution_convert_fusion = bf16[832,1728]{1,0:T(8,128)(2,1)} fusion(bf16[832,1152]{1,0:T(8,128)(2,1)S(1)} %bitcast.123, bf16[1152,1728]{0,1:T(8,128)(2,1)S(1)} %copy-done.6), kind=kOutput, calls=%fused_computation.17 | convolution fusion | flops 3313889280 | bytes 8773632 | tf_op jit(solution)/shard_map/dot_general | solution.py:46
  63.4 9.2 %reshape.348 = bf16[13,64,3,8,72]{4,3,2,1,0:T(8,128)(2,1)} reshape(bf16[832,1728]{1,0:T(8,128)(2,1)} %convolution_convert_fusion) | data formatting | bytes 5750784 | tf_op jit(solution)/shard_map/reshape | solution.py:23
  72.6 2.8 fusion.45
  75.4 1.0 fusion.23
  76.4 5.0 %fusion.48 = (f32[13,8,64]{2,1,0:T(8,128)S(1)}, f32[13,8,64,64]{2,3,1,0:T(8,128)S(1)}) fusion(f32[13,8,64,64]{2,3,1,0:T(8,128)S(1)} %fusion.23), kind=kOutput, calls=%fused_computation.116 | output fusion | flops 1703999 | bytes 3434496 | tf_op jit(solution)/shard_map/sub | solution.py:32
  81.5 0.9 fusion.26
  82.3 2.6 copy.88
  84.9 3.8 %dot_general.29 = bf16[13,64,576]{2,1,0:T(8,128)(2,1)} reshape(bf16[13,64,8,72]{3,2,1,0:T(8,128)(2,1)} %copy.88) | data formatting | bytes 1916928 | tf_op jit(solution)/shard_map/dot_general | solution.py:50
  88.8 4.3 %fusion.8 = bf16[13,64,1152]{2,1,0:T(8,128)(2,1)} fusion(bf16[13,64,576]{2,1,0:T(8,128)(2,1)} %dot_general.29, bf16[13,64,1152]{2,1,0:T(8,128)(2,1)S(1)} %copy-done.2, f32[13,1152]{1,0:T(8,128)S(1)} %bitcast.124, bf16[576,1152]{1,0:T(8,128)(2,1)S(1)} %copy-done), kind=kOutput, calls=%fused_computation.16 | convolution fusion | flops 1107984384 | bytes 6179328 | tf_op jit(solution)/shard_map/dot_general | solution.py:50
  93.1 4.8 %gather_fusion.1 = bf16[32,64,1152]{2,1,0:T(8,128)(2,1)} fusion(bf16[13,64,1152]{2,1,0:T(8,128)(2,1)} %fusion.8, s32[1024]{0:T(1024)S(1)} %pad_clamp_fusion.1), kind=kCustom, calls=%fused_computation.1 | custom fusion | bytes 9437312 | tf_op jit(solution)/shard_map/jit(_take)/gather | solution.py:90
  97.8 5.0 %broadcast_select_fusion = bf16[32,64,1152]{2,1,0:T(8,128)(2,1)} fusion(bf16[32,64,1152]{2,1,0:T(8,128)(2,1)} %gather_fusion.1, pred[32]{0:T(512)(128)(4,1)S(1)} %compare_and_fusion.2), kind=kLoop, calls=%fused_computation.8 | loop fusion | flops 2359296 | bytes 9437216 | tf_op jit(solution)/shard_map/jit(_take)/select_n | solution.py:90
  102.9 5.7 %all-to-all-start = ((bf16[32,64,1152]{2,1,0:T(8,128)(2,1)}), bf16[32,64,1152]{2,1,0:T(8,128)(2,1)}, u32[]{:S(2)}, u32[]{:S(2)}) async-start(bf16[32,64,1152]{2,1,0:T(8,128)(2,1)} %broadcast_select_fusion), calls=%async_computation | async-start | bytes 9437184 | tf_op jit(solution)/shard_map/all_to_all | solution.py:91
  108.8 93.4 %all-to-all-done = bf16[32,64,1152]{2,1,0:T(8,128)(2,1)} async-done(((bf16[32,64,1152]{2,1,0:T(8,128)(2,1)}), bf16[32,64,1152]{2,1,0:T(8,128)(2,1)}, u32[]{:S(2)}, u32[]{:S(2)}) %all-to-all-start) | async-done | bytes 4718624 | tf_op jit(solution)/shard_map/all_to_all | solution.py:91
  202.2 3.0 %gather_fusion.2 = bf16[7,64,1152]{2,1,0:T(8,128)(2,1)S(1)} fusion(bf16[32,64,1152]{2,1,0:T(8,128)(2,1)} %all-to-all-done, s32[1024]{0:T(1024)S(1)} %pad_clamp_fusion), kind=kCustom, calls=%fused_computation.2 | custom fusion | bytes 2064412 | tf_op jit(solution)/shard_map/jit(_take)/gather | solution.py:98
  205.3 1.3 copy_select_fusion
  206.5 18.9 %all-to-all-start.1 = ((bf16[7,8,8,1152]{3,2,0,1:T(8,128)(2,1)}), bf16[7,8,8,1152]{3,2,0,1:T(8,128)(2,1)S(1)}, u32[]{:S(2)}, u32[]{:S(2)}) async-start(bf16[7,8,8,1152]{3,2,0,1:T(8,128)(2,1)} %copy_select_fusion), calls=%async_computation.1 | async-start | bytes 2064384 | tf_op jit(solution)/shard_map/all_to_all | solution.py:105
  225.5 14.7 %all-to-all-done.1 = bf16[7,8,8,1152]{3,2,0,1:T(8,128)(2,1)S(1)} async-done(((bf16[7,8,8,1152]{3,2,0,1:T(8,128)(2,1)}), bf16[7,8,8,1152]{3,2,0,1:T(8,128)(2,1)S(1)}, u32[]{:S(2)}, u32[]{:S(2)}) %all-to-all-start.1) | async-done | bytes 1032224 | tf_op jit(solution)/shard_map/all_to_all | solution.py:105
  241.6 4.4 %fusion.15 = bf16[56,8,1728]{2,1,0:T(8,128)(2,1)S(1)} fusion(bf16[448,1152]{1,0:T(8,128)(2,1)S(1)} %fusion.19, bf16[1152,1728]{0,1:T(8,128)(2,1)} %param.14), kind=kOutput, calls=%fused_computation.27 | convolution fusion | flops 1784401920 | bytes 6561792 | tf_op jit(solution)/shard_map/dot_general | solution.py:108
  246.3 4.0 %reshape_reshape.6 = bf16[8,56,3,8,72]{4,3,2,1,0:T(8,128)(2,1)} reshape(bf16[8,56,1728]{2,1,0:T(8,128)(2,1)S(1)} %bitcast.120) | data formatting | bytes 3096576 | tf_op jit(solution)/shard_map/reshape;reshape | solution.py:23
  250.2 2.9 %fusion.46 = (bf16[8,56,1,8,72]{4,3,2,1,0:T(8,128)(2,1)S(1)}, bf16[8,56,1,8,72]{4,3,2,1,0:T(8,128)(2,1)S(1)}, bf16[8,56,1,8,72]{4,3,2,1,0:T(8,128)(2,1)}) fusion(bf16[8,56,3,8,72]{4,3,2,1,0:T(8,128)(2,1)} %reshape_reshape.6), kind=kLoop, calls=%fused_computation.114 | loop fusion | bytes 3096576 | tf_op jit(solution)/shard_map/slice | solution.py:35
  253.1 3.5 %fusion.49 = (f32[8,8,56]{2,1,0:T(8,128)S(1)}, f32[8,8,56,56]{2,3,1,0:T(8,128)}) fusion(bf16[8,56,1,8,72]{4,3,2,1,0:T(8,128)(2,1)} %get-tuple-element.15, bf16[8,56,1,8,72]{4,3,2,1,0:T(8,128)(2,1)S(1)} %get-tuple-element.14), kind=kOutput, calls=%fused_computation.117 | convolution fusion | flops 29503544 | bytes 1849344 | tf_op jit(solution)/shard_map/sub | solution.py:32
  256.6 2.2 fusion.27
  259.8 1.2 copy-done.3
  261.0 1.1 fusion.14
  262.0 18.2 %all_to_all.29 = bf16[56,1,8,1152]{3,2,1,0:T(8,128)(2,1)S(1)} all-to-all(bf16[56,1,8,1152]{3,2,1,0:T(8,128)(2,1)S(1)} %fusion.14), channel_id=1, replica_groups=mesh['dp'=32,'seq'=8] {'seq'}, dimensions={0} | all-to-all | bytes 2064384 | tf_op jit(solution)/shard_map/all_to_all | solution.py:129
  280.2 1.1 copy.164
  (51 shorter events, 6.0 us)
Async XLA Ops:
  0.0 88.8 %copy-start = (bf16[576,1152]{1,0:T(8,128)(2,1)S(1)}, bf16[576,1152]{1,0:T(8,128)(2,1)}, u32[]{:S(2)}) copy-start(bf16[576,1152]{1,0:T(8,128)(2,1)} %param.13) | copy-start | bytes 3981316
  0.0 54.8 %copy-start.2 = (bf16[13,64,1152]{2,1,0:T(8,128)(2,1)S(1)}, bf16[13,64,1152]{2,1,0:T(8,128)(2,1)}, u32[]{:S(2)}) copy-start(bf16[13,64,1152]{2,1,0:T(8,128)(2,1)} %param.8) | copy-start | bytes 5750788
  55.8 2.1 copy-start.6
  102.9 5.7 %copy-start.5 = (s32[32,13]{0,1:T(8,128)S(1)}, s32[32,13]{0,1:T(8,128)}, u32[]{:S(2)}) copy-start(s32[32,13]{0,1:T(8,128)} %param.11) | copy-start | bytes 4996
  102.9 99.3 %all-to-all-start = ((bf16[32,64,1152]{2,1,0:T(8,128)(2,1)}), bf16[32,64,1152]{2,1,0:T(8,128)(2,1)}, u32[]{:S(2)}, u32[]{:S(2)}) async-start(bf16[32,64,1152]{2,1,0:T(8,128)(2,1)} %broadcast_select_fusion), calls=%async_computation | async-start | bytes 9437184 | tf_op jit(solution)/shard_map/all_to_all | solution.py:91
  205.2 20.2 %copy-start.4 = (f32[1,6,1152]{2,0,1:T(1,128)S(1)}, f32[1,6,1152]{2,0,1:T(1,128)}, u32[]{:S(2)}) copy-start(f32[1,6,1152]{2,0,1:T(1,128)} %param.9) | copy-start | bytes 82948
  206.5 33.7 %all-to-all-start.1 = ((bf16[7,8,8,1152]{3,2,0,1:T(8,128)(2,1)}), bf16[7,8,8,1152]{3,2,0,1:T(8,128)(2,1)S(1)}, u32[]{:S(2)}, u32[]{:S(2)}) async-start(bf16[7,8,8,1152]{3,2,0,1:T(8,128)(2,1)} %copy_select_fusion), calls=%async_computation.1 | async-start | bytes 2064384 | tf_op jit(solution)/shard_map/all_to_all | solution.py:105
  259.6 1.3 copy-start.3
  261.0 20.3 %copy-start.1 = (bf16[576,1152]{1,0:T(8,128)(2,1)S(1)}, bf16[576,1152]{1,0:T(8,128)(2,1)}, u32[]{:S(2)}) copy-start(bf16[576,1152]{1,0:T(8,128)(2,1)} %param.13) | copy-start | bytes 3981316
where the time goes:
time: 282 us; the launch traced here: 281 us
  waiting for transfers between devices  108 us (38%)
  blocking collectives  66.1 us (23%)
  local copies, waits for them, and re-layouts  41.4 us (15%)
  starting transfers between devices  24.6 us (9%)
  matrix products  22.7 us (8%)
  other arithmetic  18.1 us (6%)
    all_to_all x1, waiting for transfers between devices, on_device(): lax.all_to_all(payload, 'dp', split_axis=0, concat_axis=0, tiled=True)  93.4 us
    all_gather x1, blocking collectives, on_device(): video_rows = lax.all_gather(modulation, 'dp', axis=0, tiled=True)  47.9 us
    all_to_all x1, starting transfers between devices, on_device(): lax.all_to_all(selected, 'seq', split_axis=1, concat_axis=0, tiled=True)  18.9 us
    all_to_all x1, blocking collectives, on_device(): lax.all_to_all(homeward.reshape(frame_total, 1, widest, back_width), 'seq...  18.2 us
    all_to_all x1, waiting for transfers between devices, on_device(): lax.all_to_all(selected, 'seq', split_axis=1, concat_axis=0, tiled=True)  14.7 us
    reshape x1, local copies, waits for them, and re-layouts, attention(): parts = qkv_rows.reshape(batch_count, length, 3, HEADS, HEAD_DIM)  9.25 us
    all_to_all x1, starting transfers between devices, on_device(): lax.all_to_all(payload, 'dp', split_axis=0, concat_axis=0, tiled=True)  5.69 us
    slice x2, local copies, waits for them, and re-layouts, attention(): parts[:, :, 2]  5.66 us
  transfers between devices with their start and end apart: 2, of which 2 were waited for; matrix products, arithmetic and copies ran while one was open for 0% of the time, Pallas kernels for 0%

commit v1 on v0

--- a/solution.py
+++ b/solution.py
@@ -84,7 +84,9 @@
         & (own_rank[:, None, None] == room_ids[None, None, :])
     )
     chosen_slot = jnp.sum(picks.astype(jnp.int32) * slot_ids[:, None, None], axis=0).reshape(-1)
-    video_rows = lax.all_gather(modulation, "dp", axis=0, tiled=True)
+    video_rows = jnp.concatenate(
+        lax.all_to_all(jnp.stack([modulation] * lax.axis_size("dp")), "dp", 0, 0), axis=0
+    )
     slot_modulation = jnp.take(video_rows, own_target, axis=0)
     processed = spatial_block(slot_tokens, slot_modulation, qkv_spatial, out_spatial)
     payload = jnp.take(processed, chosen_slot, axis=0)

time: 282 us -> 270 us (0.957)
  blocking collectives: 66.1 us -> 18.2 us
  waiting for transfers between devices: 108 us -> 139 us
  local copies, waits for them, and re-layouts: 41.4 us -> 45.2 us
    all_gather x1 -> x0, blocking collectives: 47.9 us -> none  [on_device(): video_rows = lax.all_gather(modulation, 'dp', axis=0, tiled=True)]
    all_to_all x0 -> x1, waiting for transfers between devices: none -> 21.2 us  [on_device(): lax.all_to_all(jnp.stack([modulation] * lax.axis_size('dp')), 'dp', 0, 0)]
    all_to_all x0 -> x1, starting transfers between devices: none -> 12.1 us  [on_device(): lax.all_to_all(jnp.stack([modulation] * lax.axis_size('dp')), 'dp', 0, 0)]
    all_to_all x1, starting transfers between devices: 18.9 us -> 6.99 us  [on_device(): lax.all_to_all(selected, 'seq', split_axis=1, concat_axis=0, tiled=True)]
    all_to_all x1, waiting for transfers between devices: 93.4 us -> 103 us  [on_device(): lax.all_to_all(payload, 'dp', split_axis=0, concat_axis=0, tiled=True)]
  transfers between devices with their start and end apart: 2 -> 3, of which waited for: 2 -> 3; matrix products, arithmetic and copies ran while one was open for 0% -> 1% of each run, Pallas kernels for 0% -> 0%
where the time goes in v1:
time: 270 us; the launch traced here: 268 us
  waiting for transfers between devices  139 us (51%)
  local copies, waits for them, and re-layouts  45.2 us (17%)
  starting transfers between devices  25.2 us (9%)
  matrix products  22.7 us (8%)
  blocking collectives  18.2 us (7%)
  other arithmetic  16.6 us (6%)
    all_to_all x1, waiting for transfers between devices, on_device(): lax.all_to_all(payload, 'dp', split_axis=0, concat_axis=0, tiled=True)  103 us
    all_to_all x1, waiting for transfers between devices, on_device(): lax.all_to_all(jnp.stack([modulation] * lax.axis_size('dp')), 'dp', 0, 0)  21.2 us
    all_to_all x1, blocking collectives, on_device(): lax.all_to_all(homeward.reshape(frame_total, 1, widest, back_width), 'seq...  18.2 us
    all_to_all x1, waiting for transfers between devices, on_device(): lax.all_to_all(selected, 'seq', split_axis=1, concat_axis=0, tiled=True)  14.7 us
    all_to_all x1, starting transfers between devices, on_device(): lax.all_to_all(jnp.stack([modulation] * lax.axis_size('dp')), 'dp', 0, 0)  12.1 us
    reshape x1, local copies, waits for them, and re-layouts, attention(): parts = qkv_rows.reshape(batch_count, length, 3, HEADS, HEAD_DIM)  9.25 us
    all_to_all x1, starting transfers between devices, on_device(): lax.all_to_all(selected, 'seq', split_axis=1, concat_axis=0, tiled=True)  6.99 us
    all_to_all x1, starting transfers between devices, on_device(): lax.all_to_all(payload, 'dp', split_axis=0, concat_axis=0, tiled=True)  6.09 us
  transfers between devices with their start and end apart: 3, of which 3 were waited for; matrix products, arithmetic and copies ran while one was open for 1% of the time, Pallas kernels for 0%

profile of v1, /device:TPU:1, one launch (start us, length us, event | category | flops | bytes accessed | tf_op | source)
XLA Modules:
  0.0 267.6 jit_solution(4942180043503981817)
XLA Ops:
  0.9 1.4 stack.2
  2.3 12.1 %all-to-all-start = ((f32[32,1,6,1152]{3,1,2,0:T(1,128)}), f32[32,1,6,1152]{3,1,2,0:T(1,128)}, u32[]{:S(2)}, u32[]{:S(2)}) async-start(f32[32,1,6,1152]{3,1,2,0:T(1,128)} %stack.2), calls=%async_computation | async-start | bytes 1769472 | tf_op jit(solution)/shard_map/all_to_all | solution.py:88
  16.2 21.2 %all-to-all-done = f32[32,1,6,1152]{3,1,2,0:T(1,128)} async-done(((f32[32,1,6,1152]{3,1,2,0:T(1,128)}), f32[32,1,6,1152]{3,1,2,0:T(1,128)}, u32[]{:S(2)}, u32[]{:S(2)}) %all-to-all-start) | async-done | bytes 884768 | tf_op jit(solution)/shard_map/all_to_all | solution.py:88
  37.4 2.3 copy.193
  39.7 2.6 gather_fusion
  42.3 1.1 broadcast_select_fusion.1
  44.6 1.1 copy-done.7
  45.7 5.4 %convolution_convert_fusion = bf16[832,1728]{1,0:T(8,128)(2,1)} fusion(bf16[832,1152]{1,0:T(8,128)(2,1)S(1)} %bitcast.131, bf16[1152,1728]{0,1:T(8,128)(2,1)S(1)} %copy-done.7), kind=kOutput, calls=%fused_computation.17 | convolution fusion | flops 3313889280 | bytes 8773632 | tf_op jit(solution)/shard_map/dot_general | solution.py:46
  51.2 9.2 %reshape.355 = bf16[13,64,3,8,72]{4,3,2,1,0:T(8,128)(2,1)} reshape(bf16[832,1728]{1,0:T(8,128)(2,1)} %convolution_convert_fusion) | data formatting | bytes 5750784 | tf_op jit(solution)/shard_map/reshape | solution.py:23
  60.4 2.8 %fusion.45 = (bf16[13,64,1,8,72]{4,3,2,1,0:T(8,128)(2,1)S(1)}, bf16[13,64,1,8,72]{4,3,2,1,0:T(8,128)(2,1)S(1)}, bf16[13,64,1,8,72]{4,3,2,1,0:T(8,128)(2,1)S(1)}) fusion(bf16[13,64,3,8,72]{4,3,2,1,0:T(8,128)(2,1)} %reshape.355), kind=kLoop, calls=%fused_computation.115 | loop fusion | bytes 5750784 | tf_op jit(solution)/shard_map/slice | solution.py:35
  63.2 1.0 fusion.23
  64.2 5.0 %fusion.48 = (f32[13,8,64]{2,1,0:T(8,128)S(1)}, f32[13,8,64,64]{2,3,1,0:T(8,128)S(1)}) fusion(f32[13,8,64,64]{2,3,1,0:T(8,128)S(1)} %fusion.23), kind=kOutput, calls=%fused_computation.118 | output fusion | flops 1703999 | bytes 3434496 | tf_op jit(solution)/shard_map/sub | solution.py:32
  70.1 2.6 copy.113
  72.7 3.8 %dot_general.29 = bf16[13,64,576]{2,1,0:T(8,128)(2,1)} reshape(bf16[13,64,8,72]{3,2,1,0:T(8,128)(2,1)} %copy.113) | data formatting | bytes 1916928 | tf_op jit(solution)/shard_map/dot_general | solution.py:50
  76.6 4.3 %fusion.8 = bf16[13,64,1152]{2,1,0:T(8,128)(2,1)} fusion(bf16[13,64,576]{2,1,0:T(8,128)(2,1)} %dot_general.29, bf16[13,64,1152]{2,1,0:T(8,128)(2,1)S(1)} %copy-done.2, f32[13,1152]{1,0:T(8,128)S(1)} %bitcast.133, bf16[576,1152]{1,0:T(8,128)(2,1)S(1)} %copy-done), kind=kOutput, calls=%fused_computation.16 | convolution fusion | flops 1107984384 | bytes 6179328 | tf_op jit(solution)/shard_map/dot_general | solution.py:50
  80.8 4.8 %gather_fusion.1 = bf16[32,64,1152]{2,1,0:T(8,128)(2,1)} fusion(bf16[13,64,1152]{2,1,0:T(8,128)(2,1)} %fusion.8, s32[1024]{0:T(1024)S(1)} %pad_clamp_fusion.1), kind=kCustom, calls=%fused_computation.1 | custom fusion | bytes 9437312 | tf_op jit(solution)/shard_map/jit(_take)/gather | solution.py:92
  85.6 5.0 %broadcast_select_fusion = bf16[32,64,1152]{2,1,0:T(8,128)(2,1)} fusion(bf16[32,64,1152]{2,1,0:T(8,128)(2,1)} %gather_fusion.1, pred[32]{0:T(512)(128)(4,1)S(1)} %compare_and_fusion.2), kind=kLoop, calls=%fused_computation.8 | loop fusion | flops 2359296 | bytes 9437216 | tf_op jit(solution)/shard_map/jit(_take)/select_n | solution.py:92
  90.6 6.1 %all-to-all-start.1 = ((bf16[32,64,1152]{2,1,0:T(8,128)(2,1)}), bf16[32,64,1152]{2,1,0:T(8,128)(2,1)}, u32[]{:S(2)}, u32[]{:S(2)}) async-start(bf16[32,64,1152]{2,1,0:T(8,128)(2,1)} %broadcast_select_fusion), calls=%async_computation.1 | async-start | bytes 9437184 | tf_op jit(solution)/shard_map/all_to_all | solution.py:93
  97.0 103.4 %all-to-all-done.1 = bf16[32,64,1152]{2,1,0:T(8,128)(2,1)} async-done(((bf16[32,64,1152]{2,1,0:T(8,128)(2,1)}), bf16[32,64,1152]{2,1,0:T(8,128)(2,1)}, u32[]{:S(2)}, u32[]{:S(2)}) %all-to-all-start.1) | async-done | bytes 4718624 | tf_op jit(solution)/shard_map/all_to_all | solution.py:93
  200.4 3.0 %gather_fusion.2 = bf16[7,64,1152]{2,1,0:T(8,128)(2,1)S(1)} fusion(bf16[32,64,1152]{2,1,0:T(8,128)(2,1)} %all-to-all-done.1, s32[1024]{0:T(1024)S(1)} %pad_clamp_fusion), kind=kCustom, calls=%fused_computation.2 | custom fusion | bytes 2064412 | tf_op jit(solution)/shard_map/jit(_take)/gather | solution.py:100
  203.4 1.3 copy_select_fusion
  204.7 7.0 %all-to-all-start.2 = ((bf16[7,8,8,1152]{3,2,0,1:T(8,128)(2,1)}), bf16[7,8,8,1152]{3,2,0,1:T(8,128)(2,1)S(1)}, u32[]{:S(2)}, u32[]{:S(2)}) async-start(bf16[7,8,8,1152]{3,2,0,1:T(8,128)(2,1)} %copy_select_fusion), calls=%async_computation.2 | async-start | bytes 2064384 | tf_op jit(solution)/shard_map/all_to_all | solution.py:107
  211.8 14.7 %all-to-all-done.2 = bf16[7,8,8,1152]{3,2,0,1:T(8,128)(2,1)S(1)} async-done(((bf16[7,8,8,1152]{3,2,0,1:T(8,128)(2,1)}), bf16[7,8,8,1152]{3,2,0,1:T(8,128)(2,1)S(1)}, u32[]{:S(2)}, u32[]{:S(2)}) %all-to-all-start.2) | async-done | bytes 1032224 | tf_op jit(solution)/shard_map/all_to_all | solution.py:107
  227.9 4.4 %fusion.15 = bf16[56,8,1728]{2,1,0:T(8,128)(2,1)S(1)} fusion(bf16[448,1152]{1,0:T(8,128)(2,1)S(1)} %fusion.19, bf16[1152,1728]{0,1:T(8,128)(2,1)} %param.14), kind=kOutput, calls=%fused_computation.27 | convolution fusion | flops 1784401920 | bytes 6561792 | tf_op jit(solution)/shard_map/dot_general | solution.py:110
  232.5 4.0 %reshape_reshape.6 = bf16[8,56,3,8,72]{4,3,2,1,0:T(8,128)(2,1)} reshape(bf16[8,56,1728]{2,1,0:T(8,128)(2,1)S(1)} %bitcast.127) | data formatting | bytes 3096576 | tf_op jit(solution)/shard_map/reshape;reshape | solution.py:23
  236.5 2.9 %fusion.46 = (bf16[8,56,1,8,72]{4,3,2,1,0:T(8,128)(2,1)S(1)}, bf16[8,56,1,8,72]{4,3,2,1,0:T(8,128)(2,1)S(1)}, bf16[8,56,1,8,72]{4,3,2,1,0:T(8,128)(2,1)}) fusion(bf16[8,56,3,8,72]{4,3,2,1,0:T(8,128)(2,1)} %reshape_reshape.6), kind=kLoop, calls=%fused_computation.116 | loop fusion | bytes 3096576 | tf_op jit(solution)/shard_map/slice | solution.py:35
  239.4 3.5 %fusion.49 = (f32[8,8,56]{2,1,0:T(8,128)S(1)}, f32[8,8,56,56]{2,3,1,0:T(8,128)}) fusion(bf16[8,56,1,8,72]{4,3,2,1,0:T(8,128)(2,1)} %get-tuple-element.15, bf16[8,56,1,8,72]{4,3,2,1,0:T(8,128)(2,1)S(1)} %get-tuple-element.14), kind=kOutput, calls=%fused_computation.119 | convolution fusion | flops 29503544 | bytes 1849344 | tf_op jit(solution)/shard_map/sub | solution.py:32
  242.9 2.2 fusion.27
  246.1 1.2 copy-done.3
  247.2 1.1 fusion.14
  248.3 18.2 %all_to_all.34 = bf16[56,1,8,1152]{3,2,1,0:T(8,128)(2,1)S(1)} all-to-all(bf16[56,1,8,1152]{3,2,1,0:T(8,128)(2,1)S(1)} %fusion.14), channel_id=1, replica_groups=mesh['dp'=32,'seq'=8] {'seq'}, dimensions={0} | all-to-all | bytes 2064384 | tf_op jit(solution)/shard_map/all_to_all | solution.py:131
  266.5 1.1 copy.194
  (56 shorter events, 7.4 us)
Async XLA Ops:
  0.0 76.6 %copy-start = (bf16[576,1152]{1,0:T(8,128)(2,1)S(1)}, bf16[576,1152]{1,0:T(8,128)(2,1)}, u32[]{:S(2)}) copy-start(bf16[576,1152]{1,0:T(8,128)(2,1)} %param.13) | copy-start | bytes 3981316
  0.0 14.5 %copy-start.5 = (s32[32,13]{0,1:T(8,128)S(1)}, s32[32,13]{0,1:T(8,128)}, u32[]{:S(2)}) copy-start(s32[32,13]{0,1:T(8,128)} %param.11) | copy-start | bytes 4996
  0.0 14.7 %copy-start.6 = (s32[32]{0:T(128)S(1)}, s32[32]{0:T(128)}, u32[]{:S(2)}) copy-start(s32[32]{0:T(128)} %param.10) | copy-start | bytes 388
  0.0 15.2 %copy-start.2 = (bf16[13,64,1152]{2,1,0:T(8,128)(2,1)S(1)}, bf16[13,64,1152]{2,1,0:T(8,128)(2,1)}, u32[]{:S(2)}) copy-start(bf16[13,64,1152]{2,1,0:T(8,128)(2,1)} %param.8) | copy-start | bytes 5750788
  2.3 35.1 %all-to-all-start = ((f32[32,1,6,1152]{3,1,2,0:T(1,128)}), f32[32,1,6,1152]{3,1,2,0:T(1,128)}, u32[]{:S(2)}, u32[]{:S(2)}) async-start(f32[32,1,6,1152]{3,1,2,0:T(1,128)} %stack.2), calls=%async_computation | async-start | bytes 1769472 | tf_op jit(solution)/shard_map/all_to_all | solution.py:88
  43.6 2.1 copy-start.7
  90.6 109.7 %all-to-all-start.1 = ((bf16[32,64,1152]{2,1,0:T(8,128)(2,1)}), bf16[32,64,1152]{2,1,0:T(8,128)(2,1)}, u32[]{:S(2)}, u32[]{:S(2)}) async-start(bf16[32,64,1152]{2,1,0:T(8,128)(2,1)} %broadcast_select_fusion), calls=%async_computation.1 | async-start | bytes 9437184 | tf_op jit(solution)/shard_map/all_to_all | solution.py:93
  203.4 8.3 %copy-start.4 = (f32[1,6,1152]{2,0,1:T(1,128)S(1)}, f32[1,6,1152]{2,0,1:T(1,128)}, u32[]{:S(2)}) copy-start(f32[1,6,1152]{2,0,1:T(1,128)} %param.9) | copy-start | bytes 82948
  204.7 21.8 %all-to-all-start.2 = ((bf16[7,8,8,1152]{3,2,0,1:T(8,128)(2,1)}), bf16[7,8,8,1152]{3,2,0,1:T(8,128)(2,1)S(1)}, u32[]{:S(2)}, u32[]{:S(2)}) async-start(bf16[7,8,8,1152]{3,2,0,1:T(8,128)(2,1)} %copy_select_fusion), calls=%async_computation.2 | async-start | bytes 2064384 | tf_op jit(solution)/shard_map/all_to_all | solution.py:107
  245.9 1.3 copy-start.3
  247.2 20.3 %copy-start.1 = (bf16[576,1152]{1,0:T(8,128)(2,1)S(1)}, bf16[576,1152]{1,0:T(8,128)(2,1)}, u32[]{:S(2)}) copy-start(bf16[576,1152]{1,0:T(8,128)(2,1)} %param.13) | copy-start | bytes 3981316
